TPU v7x, 512 devices: a whole 4x8x8 slice. The times are simulated.
512 devices in a mesh: ctx: 64 (over y_hi, x, z), exp: 8 (over y_lo, core).
Axes of the slice: x: 4, y: 8 (y_hi: 2, y_lo: 4; y = y_hi * 4 + y_lo), z: 8, core: 2. Of those that a mesh axis runs over, the one named last changes fastest.
Arguments:
- queries: bfloat16 [4096, 6144], P('ctx', 'exp'), may hold values from -5 to 5
- keys: bfloat16 [4096, 1024], P('ctx', 'exp'), may hold values from -5 to 5
- values: bfloat16 [4096, 1024], P('ctx', 'exp'), may hold values from -16 to 16
- residual: bfloat16 [4096, 6144], P('ctx', 'exp'), may hold values from -25 to 25
- norm_gain: float32 [6144], P('exp'), may hold values from 0.5 to 1.5
- routes: int32 [4096, 1], P('ctx'), may hold values from 0 to 3; in each aligned block of 64 rows (0 to 63, 64 to 127, ...) at most 24 rows name the same one
- route_weight: float32 [4096], P('ctx'), may hold values from 0.25 to 1
- w_gate: bfloat16 [65536, 6144], P('ctx', 'exp'), may hold values from -0.078125 to 0.078125
- w_up: bfloat16 [65536, 6144], P('ctx', 'exp'), may hold values from -0.078125 to 0.078125
- w_down: bfloat16 [65536, 6144], P('ctx', 'exp'), may hold values from -0.046875 to 0.046875
Outputs:
- moe_out: bfloat16 [4096, 6144], P('ctx', 'exp')
Inputs may be any that keep to these rules, and one draw needn't show every extreme that they name: `routes`: within the 64 rows of one device, at most 24 tokens have the same route.
All inputs are finite; a program needn't handle non-finite values.
Results may differ from a plain program's by a relative error of at most 0.029.
Values may be sent and summed in bfloat16 or wider, within the bound.
No kernel may reach another device: no remote copies, remote signals or barrier semaphores. Data moves between devices by JAX's collectives and lax.ppermute only.
A program may use at most 64 MiB of HBM per device.

v0:
```python
import math
import jax
import jax.numpy as jnp
from jax import lax
from jax.sharding import Mesh, PartitionSpec as P

D = 6144
HD = 128
EXPERTS = 4
CAP = 24
CHUNKS = 2
F32 = jnp.float32
BF16 = jnp.bfloat16
CTX = ("yh", "xh", "xl", "z")
EXP = ("yl", "c")
HALF = ("xh", "xl", "z")
SWAP = [(0, 1), (1, 0)]
Y_XOR = [[(i, i ^ k) for i in range(4)] for k in range(4)]


def swap(x, axis):
    return lax.ppermute(x, axis, SWAP)


def split3(v):
    hi = lax.reduce_precision(v, 8, 7)
    mid = lax.reduce_precision(v - hi, 8, 7)
    lo = v - hi - mid
    return [p.astype(BF16) for p in (hi, mid, lo)]


def attend(queries, keys, values):
    rows = queries.shape[0]
    heads = queries.shape[1] // HD
    yh = lax.axis_index("yh")
    scale = 1.0 / math.sqrt(HD)
    foreign = lax.ppermute(queries, "yh", [(1, 0)])
    kv = jnp.concatenate([keys, values], axis=1)
    members = lax.axis_size(HALF)
    kv = lax.all_to_all(
        jnp.broadcast_to(kv[None], (members,) + kv.shape),
        HALF,
        split_axis=0,
        concat_axis=0,
        tiled=True,
    ).reshape(members * rows, 2 * HD)
    k_all, v_all = (kv[:, :HD], kv[:, HD:])
    count = members * rows

    def stacked(q):
        return q.reshape(rows, heads, HD).transpose(1, 0, 2).reshape(heads * rows, HD)

    q_all = jnp.concatenate([stacked(queries), stacked(foreign)], axis=0)
    own_pos = lax.axis_index(HALF) * rows + jnp.tile(jnp.arange(rows, dtype=jnp.int32), heads)
    limit = jnp.concatenate([own_pos, jnp.full_like(own_pos, count)])
    scores = jnp.einsum("qd,kd->qk", q_all, k_all, preferred_element_type=F32) * scale
    allowed = jnp.arange(count, dtype=jnp.int32)[None, :] <= limit[:, None]
    scores = jnp.where(allowed, scores, -1e30)
    top = jnp.max(scores, axis=1)
    weights = jnp.exp(scores - top[:, None])
    total = jnp.sum(weights, axis=1)
    acc = jnp.einsum("qk,kd->qd", weights.astype(BF16), v_all, preferred_element_type=F32)
    out = acc / total[:, None]
    lse = top + jnp.log(total)
    n = heads * rows

    def unstacked(o):
        return o.reshape(heads, rows, HD).transpose(1, 0, 2).reshape(rows, heads * HD)

    out_own, out_far = (unstacked(out[:n]), unstacked(out[n:]))
    lse_own, lse_far = (lse[:n].reshape(heads, rows).T, lse[n:].reshape(heads, rows).T)
    tail = jnp.concatenate(split3(lse_far), axis=1)
    tail = jnp.pad(tail, ((0, 0), (0, HD - tail.shape[1])))
    message = jnp.concatenate([out_far.astype(BF16), tail], axis=1)
    got = lax.ppermute(message, "yh", [(0, 1)])
    got_out = got[:, : heads * HD].astype(F32)
    parts = got[:, heads * HD : heads * HD + 3 * heads].astype(F32)
    got_lse = parts[:, :heads] + parts[:, heads : 2 * heads] + parts[:, 2 * heads :]
    share = jnp.where(yh == 1, jax.nn.sigmoid(got_lse - lse_own), 0.0)
    share = jnp.repeat(share, HD, axis=1)
    return (out_own * (1.0 - share) + got_out * share).astype(BF16)


def body(queries, keys, values, residual, norm_gain, routes, route_weight, w_gate, w_up, w_down):
    rows = queries.shape[0]
    feat = residual.shape[1]
    hidden_local = w_gate.shape[0]
    half = hidden_local // 2
    core = lax.axis_index("c")

    def halves(w, which):
        return lax.dynamic_slice_in_dim(w, which * half, half, axis=0)

    w_in = jnp.concatenate([halves(w_gate, core), halves(w_up, core)], axis=0)
    w_in_other = swap(
        jnp.concatenate([halves(w_gate, 1 - core), halves(w_up, 1 - core)], axis=0), "c"
    )
    w_out = halves(w_down, core)
    w_out_other = halves(w_down, 1 - core)
    attn = attend(queries, keys, values)
    mixed = residual.astype(F32) + attn.astype(F32)
    total_squares = lax.psum(jnp.sum(mixed * mixed, axis=1), EXP)
    normed = (mixed * lax.rsqrt(total_squares / D + 1e-05)[:, None] * norm_gain[None, :]).astype(
        BF16
    )
    chosen = routes[:, 0]
    expert_ids = jnp.arange(EXPERTS, dtype=jnp.int32)
    onehot = (chosen[:, None] == expert_ids[None, :]).astype(jnp.int32)
    slot_index = jnp.sum((jnp.cumsum(onehot, axis=0) - 1) * onehot, axis=1)
    slot_ids = jnp.arange(CAP, dtype=jnp.int32)
    select = (
        (chosen[None, None, :] == expert_ids[:, None, None])
        & (slot_index[None, None, :] == slot_ids[None, :, None])
    ).astype(BF16)
    packed = jnp.einsum("ect,td->ecd", select, normed, preferred_element_type=F32).astype(BF16)
    incoming = lax.all_to_all(packed, ("yh", "xh"), split_axis=0, concat_axis=0, tiled=True)
    nz = lax.axis_size("z")
    ny = lax.axis_size("yl")
    slots = CAP // CHUNKS
    block = EXPERTS * slots
    outs = []
    for k in range(CHUNKS):
        part = incoming[:, k * slots : (k + 1) * slots].reshape(block, feat)
        near = lax.all_to_all(
            jnp.broadcast_to(part[None], (nz, block, feat)),
            "z",
            split_axis=0,
            concat_axis=0,
            tiled=True,
        ).reshape(nz * block, feat)
        x = jnp.concatenate([near, swap(near, "xl")], axis=0)
        x_other = swap(x, "c")
        gate_up = jnp.einsum("rd,fd->rf", x, w_in, preferred_element_type=F32) + jnp.einsum(
            "rd,fd->rf", x_other, w_in_other, preferred_element_type=F32
        )
        n_rows = gate_up.shape[0]
        share = n_rows // ny
        gate_up = gate_up.astype(BF16).reshape(ny, share, 2 * half)
        me = lax.axis_index("yl")

        def piece(i):
            return lax.dynamic_index_in_dim(gate_up, me ^ i, 0, keepdims=False)

        full = piece(0).astype(F32)
        for i in range(1, ny):
            full = full + lax.ppermute(piece(i), "yl", Y_XOR[i]).astype(F32)
        hidden = (jax.nn.silu(full[:, :half]) * full[:, half:]).astype(BF16)
        hid = jnp.zeros((ny, share, half), BF16)
        hid = lax.dynamic_update_index_in_dim(hid, hidden, me, 0)
        for i in range(1, ny):
            hid = lax.dynamic_update_index_in_dim(
                hid, lax.ppermute(hidden, "yl", Y_XOR[i]), me ^ i, 0
            )
        hid = hid.reshape(n_rows, half)
        hid_other = swap(hid, "c")
        down = jnp.dot(hid, w_out, preferred_element_type=F32) + jnp.dot(
            hid_other, w_out_other, preferred_element_type=F32
        )
        stay, leave = (down[: n_rows // 2], down[n_rows // 2 :])
        summed = (stay + swap(leave.astype(BF16), "xl").astype(F32)).astype(BF16)
        back = lax.all_to_all(
            summed.reshape(nz, block, feat), "z", split_axis=0, concat_axis=0, tiled=True
        )
        outs.append(jnp.sum(back.astype(F32), axis=0).astype(BF16).reshape(EXPERTS, slots, feat))
    out = jnp.concatenate(outs, axis=1)
    returned = lax.all_to_all(out, ("yh", "xh"), split_axis=0, concat_axis=0, tiled=True)
    moe_rows = jnp.einsum("ect,ecd->td", select, returned, preferred_element_type=F32)
    return (route_weight[:, None] * moe_rows).astype(BF16)


def solution(mesh):
    fine = Mesh(mesh.devices.reshape(2, 2, 2, 8, 4, 2), CTX + EXP)
    wide = P(CTX, EXP)
    in_specs = (wide, wide, wide, wide, P(EXP), P(CTX, None), P(CTX), wide, wide, wide)
    return jax.shard_map(body, mesh=fine, in_specs=in_specs, out_specs=wide, check_vma=False)
```

profile of v0, /device:TPU:8, one launch (start us, length us, event | category | flops | bytes accessed | tf_op | source)
XLA Modules:
  0.0 368.0 jit_solution(5424616710159542530)
XLA Ops:
  2.0 13.2 %all-to-all-start = ((bf16[32,64,256]{2,1,0:T(8,128)(2,1)}), bf16[32,64,256]{2,1,0:T(8,128)(2,1)S(1)}, u32[]{:S(2)}, u32[]{:S(2)}) async-start(bf16[32,64,256]{2,1,0:T(8,128)(2,1)} %broadcast_in_dim.68), calls=%async_computation | async-start | bytes 2097152 | tf_op jit(solution)/shard_map/all_to_all | solution.py:40
  17.1 10.6 %collective-permute-done = bf16[64,768]{1,0:T(8,128)(2,1)S(1)} collective-permute-done((bf16[64,768]{1,0:T(8,128)(2,1)S(1)}, bf16[64,768]{1,0:T(8,128)(2,1)S(1)}, u32[]{:S(2)}, u32[]{:S(2)}) %collective-permute-start) | collective-permute-done | bytes 98336 | tf_op jit(solution)/shard_map/ppermute | solution.py:37
  27.8 15.9 %all-to-all-done = bf16[32,64,256]{2,1,0:T(8,128)(2,1)S(1)} async-done(((bf16[32,64,256]{2,1,0:T(8,128)(2,1)}), bf16[32,64,256]{2,1,0:T(8,128)(2,1)S(1)}, u32[]{:S(2)}, u32[]{:S(2)}) %all-to-all-start) | async-done | bytes 1048608 | tf_op jit(solution)/shard_map/all_to_all | solution.py:40
  49.4 6.8 %collective-permute-start.1 = (bf16[64,896]{1,0:T(8,128)(2,1)S(1)}, bf16[64,896]{1,0:T(8,128)(2,1)S(1)}, u32[]{:S(2)}, u32[]{:S(2)}) collective-permute-start(bf16[64,896]{1,0:T(8,128)(2,1)S(1)} %fusion.34), channel_id=1, source_target_pairs={{0,256},{1,257},{2,258},{3,259},{4,260},{5,261},{6,262},{7,263},{8... | collective-permute-start | bytes 344072 | tf_op jit(solution)/shard_map/ppermute | solution.py:75
  56.6 3.2 collective-permute-done.1
  60.2 10.0 %psum.7 = f32[64]{0:T(128)S(1)} all-reduce(f32[64]{0:T(128)S(1)} %get-tuple-element.9), channel_id=1, replica_groups=mesh['yh'=2,'xh'=2,'xl'=2,'z'=8,'yl'=4,'c'=2] {'yl','c'}, use_global_device_ids=true, to_apply=%region_5.6 | all-reduce | flops 64 | bytes 512 | tf_op jit(solution)/shard_map/psum | solution.py:102
  70.5 20.1 %all_to_all.35 = bf16[4,24,768]{2,1,0:T(8,128)(2,1)S(1)} all-to-all(bf16[4,24,768]{2,1,0:T(8,128)(2,1)S(1)} %convolution_convert_fusion), channel_id=1, replica_groups=mesh['yh'=2,'xh'=2,'xl'=2,'z'=8,'yl'=4,'c'=2] {'yh','xh'}, dimensions={0} | all-to-all | bytes 294912 | tf_op jit(solution)/shard_map/all_to_all | solution.py:116
  91.5 4.8 %all-to-all-start.2 = ((bf16[8,48,768]{2,1,0:T(8,128)(2,1)}), bf16[8,48,768]{2,1,0:T(8,128)(2,1)S(1)}, u32[]{:S(2)}, u32[]{:S(2)}) async-start(bf16[8,48,768]{2,1,0:T(8,128)(2,1)} %broadcast_in_dim.73), calls=%async_computation.2 | async-start | bytes 1179648 | tf_op jit(solution)/shard_map/all_to_all | solution.py:124
  96.3 17.9 %all-to-all-done.2 = bf16[8,48,768]{2,1,0:T(8,128)(2,1)S(1)} async-done(((bf16[8,48,768]{2,1,0:T(8,128)(2,1)}), bf16[8,48,768]{2,1,0:T(8,128)(2,1)S(1)}, u32[]{:S(2)}, u32[]{:S(2)}) %all-to-all-start.2) | async-done | bytes 589856 | tf_op jit(solution)/shard_map/all_to_all | solution.py:124
  115.1 3.5 all-to-all-start.4
  126.7 6.9 %collective-permute-done.2 = bf16[384,768]{1,0:T(8,128)(2,1)S(1)} collective-permute-done((bf16[384,768]{1,0:T(8,128)(2,1)S(1)}, bf16[384,768]{1,0:T(8,128)(2,1)S(1)}, u32[]{:S(2)}, u32[]{:S(2)}) %collective-permute-start.2) | collective-permute-done | bytes 589856 | tf_op jit(solution)/shard_map/ppermute | solution.py:22
  139.0 15.4 %collective-permute-done.13 = bf16[384,768]{1,0:T(8,128)(2,1)S(1)} collective-permute-done((bf16[384,768]{1,0:T(8,128)(2,1)S(1)}, bf16[384,768]{1,0:T(8,128)(2,1)S(1)}, u32[]{:S(2)}, u32[]{:S(2)}) %collective-permute-start.13) | collective-permute-done | bytes 589856 | tf_op jit(solution)/shard_map/ppermute | solution.py:22
  158.4 3.3 fusion.67
  166.2 3.4 collective-permute-start.6
  169.6 3.2 collective-permute-start.7
  172.8 3.2 fusion.68
  177.5 3.9 %collective-permute-start.15 = (bf16[192,1024]{1,0:T(8,128)(2,1)S(1)}, bf16[192,1024]{1,0:T(8,128)(2,1)S(1)}, u32[]{:S(2)}, u32[]{:S(2)}) collective-permute-start(bf16[192,1024]{1,0:T(8,128)(2,1)S(1)} %get-tuple-element.14), channel_id=1, source_target_pairs={{0,2},{2,0},{4,6},{6,4},{1,3},{3,1},{5,7},{7,5},{8,10},{10,8},{12,... | collective-permute-start | bytes 1179656 | tf_op jit(solution)/shard_map/ppermute | solution.py:146
  181.4 3.4 collective-permute-start.16
  187.3 8.7 %collective-permute-done.6 = bf16[192,1024]{1,0:T(8,128)(2,1)S(1)} collective-permute-done((bf16[192,1024]{1,0:T(8,128)(2,1)S(1)}, bf16[192,1024]{1,0:T(8,128)(2,1)S(1)}, u32[]{:S(2)}, u32[]{:S(2)}) %collective-permute-start.6) | collective-permute-done | bytes 393248 | tf_op jit(solution)/shard_map/ppermute | solution.py:146
  196.0 26.7 %collective-permute-done.7 = bf16[192,1024]{1,0:T(8,128)(2,1)S(1)} collective-permute-done((bf16[192,1024]{1,0:T(8,128)(2,1)S(1)}, bf16[192,1024]{1,0:T(8,128)(2,1)S(1)}, u32[]{:S(2)}, u32[]{:S(2)}) %collective-permute-start.7) | collective-permute-done | bytes 393248 | tf_op jit(solution)/shard_map/ppermute | solution.py:146
  225.1 4.4 %collective-permute-start.9 = (bf16[192,512]{1,0:T(8,128)(2,1)S(1)}, bf16[192,512]{1,0:T(8,128)(2,1)S(1)}, u32[]{:S(2)}, u32[]{:S(2)}) collective-permute-start(bf16[192,512]{1,0:T(8,128)(2,1)S(1)} %get-tuple-element.6), channel_id=1, source_target_pairs={{0,4},{2,6},{4,0},{6,2},{1,5},{3,7},{5,1},{7,3},{8,12},{10,14},{12... | collective-permute-start | bytes 589832 | tf_op jit(solution)/shard_map/ppermute | solution.py:152
  232.4 15.6 %collective-permute-done.17 = bf16[192,1024]{1,0:T(8,128)(2,1)S(1)} collective-permute-done((bf16[192,1024]{1,0:T(8,128)(2,1)S(1)}, bf16[192,1024]{1,0:T(8,128)(2,1)S(1)}, u32[]{:S(2)}, u32[]{:S(2)}) %collective-permute-start.17) | collective-permute-done | bytes 393248 | tf_op jit(solution)/shard_map/ppermute | solution.py:146
  250.8 4.9 %collective-permute-done.10 = bf16[192,512]{1,0:T(8,128)(2,1)S(1)} collective-permute-done((bf16[192,512]{1,0:T(8,128)(2,1)S(1)}, bf16[192,512]{1,0:T(8,128)(2,1)S(1)}, u32[]{:S(2)}, u32[]{:S(2)}) %collective-permute-start.10) | collective-permute-done | bytes 196640 | tf_op jit(solution)/shard_map/ppermute | solution.py:152
  259.6 3.3 collective-permute-start.20
  262.9 10.4 %collective-permute-done.19 = bf16[192,512]{1,0:T(8,128)(2,1)S(1)} collective-permute-done((bf16[192,512]{1,0:T(8,128)(2,1)S(1)}, bf16[192,512]{1,0:T(8,128)(2,1)S(1)}, u32[]{:S(2)}, u32[]{:S(2)}) %collective-permute-start.19) | collective-permute-done | bytes 196640 | tf_op jit(solution)/shard_map/ppermute | solution.py:152
  273.3 5.8 %collective-permute-done.20 = bf16[192,512]{1,0:T(8,128)(2,1)S(1)} collective-permute-done((bf16[192,512]{1,0:T(8,128)(2,1)S(1)}, bf16[192,512]{1,0:T(8,128)(2,1)S(1)}, u32[]{:S(2)}, u32[]{:S(2)}) %collective-permute-start.20) | collective-permute-done | bytes 196640 | tf_op jit(solution)/shard_map/ppermute | solution.py:152
  287.2 13.2 %collective-permute-done.12 = bf16[384,768]{1,0:T(8,128)(2,1)S(1)} collective-permute-done((bf16[384,768]{1,0:T(8,128)(2,1)S(1)}, bf16[384,768]{1,0:T(8,128)(2,1)S(1)}, u32[]{:S(2)}, u32[]{:S(2)}) %collective-permute-start.12) | collective-permute-done | bytes 589856 | tf_op jit(solution)/shard_map/ppermute | solution.py:22
  301.3 6.8 %all-to-all-start.3 = ((bf16[8,48,768]{2,1,0:T(8,128)(2,1)}), bf16[8,48,768]{2,1,0:T(8,128)(2,1)S(1)}, u32[]{:S(2)}, u32[]{:S(2)}) async-start(bf16[8,48,768]{2,1,0:T(8,128)(2,1)} %bitcast.24), calls=%async_computation.3 | async-start | bytes 1179648 | tf_op jit(solution)/shard_map/all_to_all | solution.py:161
  312.9 14.4 %collective-permute-done.22 = bf16[384,768]{1,0:T(8,128)(2,1)S(1)} collective-permute-done((bf16[384,768]{1,0:T(8,128)(2,1)S(1)}, bf16[384,768]{1,0:T(8,128)(2,1)S(1)}, u32[]{:S(2)}, u32[]{:S(2)}) %collective-permute-start.22) | collective-permute-done | bytes 589856 | tf_op jit(solution)/shard_map/ppermute | solution.py:22
  328.2 6.9 %all-to-all-start.5 = ((bf16[8,48,768]{2,1,0:T(8,128)(2,1)}), bf16[8,48,768]{2,1,0:T(8,128)(2,1)S(1)}, u32[]{:S(2)}, u32[]{:S(2)}) async-start(bf16[8,48,768]{2,1,0:T(8,128)(2,1)} %bitcast.36), calls=%async_computation.5 | async-start | bytes 1179648 | tf_op jit(solution)/shard_map/all_to_all | solution.py:161
  335.3 17.2 %all-to-all-done.5 = bf16[8,48,768]{2,1,0:T(8,128)(2,1)S(1)} async-done(((bf16[8,48,768]{2,1,0:T(8,128)(2,1)}), bf16[8,48,768]{2,1,0:T(8,128)(2,1)S(1)}, u32[]{:S(2)}, u32[]{:S(2)}) %all-to-all-start.5) | async-done | bytes 589856 | tf_op jit(solution)/shard_map/all_to_all | solution.py:161
  352.6 14.5 %all_to_all.36 = bf16[4,24,768]{2,1,0:T(8,128)(2,1)S(1)} all-to-all(bf16[4,24,768]{2,1,0:T(8,128)(2,1)S(1)} %pad_maximum_fusion.6), channel_id=1, replica_groups=mesh['yh'=2,'xh'=2,'xl'=2,'z'=8,'yl'=4,'c'=2] {'yh','xh'}, dimensions={0} | all-to-all | bytes 294912 | tf_op jit(solution)/shard_map/all_to_all | solution.py:166
  (127 shorter events, 65.8 us)
Async XLA Ops:
  0.0 281.1 %copy-start = (bf16[1024,768]{1,0:T(8,128)(2,1)S(1)}, bf16[1024,768]{1,0:T(8,128)(2,1)}, u32[]{:S(2)}) copy-start(bf16[1024,768]{1,0:T(8,128)(2,1)} %param.19) | copy-start | bytes 4718596
  0.0 16.6 %copy-start.9 = (s32[64,1]{0,1:T(1,128)S(1)}, s32[64,1]{0,1:T(1,128)}, u32[]{:S(2)}) copy-start(s32[64,1]{0,1:T(1,128)} %param.15) | copy-start | bytes 772
  2.0 41.8 %all-to-all-start = ((bf16[32,64,256]{2,1,0:T(8,128)(2,1)}), bf16[32,64,256]{2,1,0:T(8,128)(2,1)S(1)}, u32[]{:S(2)}, u32[]{:S(2)}) async-start(bf16[32,64,256]{2,1,0:T(8,128)(2,1)} %broadcast_in_dim.68), calls=%async_computation | async-start | bytes 2097152 | tf_op jit(solution)/shard_map/all_to_all | solution.py:40
  15.2 12.5 %collective-permute-start = (bf16[64,768]{1,0:T(8,128)(2,1)S(1)}, bf16[64,768]{1,0:T(8,128)(2,1)S(1)}, u32[]{:S(2)}, u32[]{:S(2)}) collective-permute-start(bf16[64,768]{1,0:T(8,128)(2,1)S(1)} %copy-done.7), channel_id=1, source_target_pairs={{256,0},{257,1},{258,2},{259,3},{260,4},{261,5},{262,6},{263,7},{2... | collective-permute-start | bytes 294920 | tf_op jit(solution)/shard_map/ppermute | solution.py:37
  49.1 21.2 %copy-start.8 = (f32[768]{0:T(1024)S(1)}, f32[768]{0:T(1024)}, u32[]{:S(2)}) copy-start(f32[768]{0:T(1024)} %param.14) | copy-start | bytes 9220
  49.4 10.4 %collective-permute-start.1 = (bf16[64,896]{1,0:T(8,128)(2,1)S(1)}, bf16[64,896]{1,0:T(8,128)(2,1)S(1)}, u32[]{:S(2)}, u32[]{:S(2)}) collective-permute-start(bf16[64,896]{1,0:T(8,128)(2,1)S(1)} %fusion.34), channel_id=1, source_target_pairs={{0,256},{1,257},{2,258},{3,259},{4,260},{5,261},{6,262},{7,263},{8... | collective-permute-start | bytes 344072 | tf_op jit(solution)/shard_map/ppermute | solution.py:75
  91.5 22.7 %all-to-all-start.2 = ((bf16[8,48,768]{2,1,0:T(8,128)(2,1)}), bf16[8,48,768]{2,1,0:T(8,128)(2,1)S(1)}, u32[]{:S(2)}, u32[]{:S(2)}) async-start(bf16[8,48,768]{2,1,0:T(8,128)(2,1)} %broadcast_in_dim.73), calls=%async_computation.2 | async-start | bytes 1179648 | tf_op jit(solution)/shard_map/all_to_all | solution.py:124
  115.1 21.7 %all-to-all-start.4 = ((bf16[8,48,768]{2,1,0:T(8,128)(2,1)}), bf16[8,48,768]{2,1,0:T(8,128)(2,1)S(1)}, u32[]{:S(2)}, u32[]{:S(2)}) async-start(bf16[8,48,768]{2,1,0:T(8,128)(2,1)} %broadcast_in_dim.79), calls=%async_computation.4 | async-start | bytes 1179648 | tf_op jit(solution)/shard_map/all_to_all | solution.py:124
  118.6 15.0 %collective-permute-start.2 = (bf16[384,768]{1,0:T(8,128)(2,1)S(1)}, bf16[384,768]{1,0:T(8,128)(2,1)S(1)}, u32[]{:S(2)}, u32[]{:S(2)}) collective-permute-start(bf16[384,768]{1,0:T(8,128)(2,1)S(1)} %bitcast.107), channel_id=1, source_target_pairs={{0,64},{64,0},{1,65},{65,1},{2,66},{66,2},{3,67},{67,3},{4,68},{68... | collective-permute-start | bytes 1769480 | tf_op jit(solution)/shard_map/ppermute | solution.py:22
  124.8 33.6 %collective-permute-start.4 = (bf16[1024,768]{1,0:T(8,128)(2,1)}, bf16[1024,768]{1,0:T(8,128)(2,1)}, u32[]{:S(2)}, u32[]{:S(2)}) collective-permute-start(bf16[1024,768]{1,0:T(8,128)(2,1)} %pad_maximum_fusion.1), channel_id=1, source_target_pairs={{0,1},{1,0},{2,3},{3,2},{4,5},{5,4},{6,7},{7,6},{8,9},{9,8},{10,11... | collective-permute-start | bytes 4718600 | tf_op jit(solution)/shard_map/ppermute | solution.py:22
  134.9 23.5 %collective-permute-start.3 = (bf16[768,768]{1,0:T(8,128)(2,1)}, bf16[768,768]{1,0:T(8,128)(2,1)}, u32[]{:S(2)}, u32[]{:S(2)}) collective-permute-start(bf16[768,768]{1,0:T(8,128)(2,1)} %pad_maximum_fusion.2), channel_id=1, source_target_pairs={{0,1},{1,0},{2,3},{3,2},{4,5},{5,4},{6,7},{7,6},{8,9},{9,8},{10,11... | collective-permute-start | bytes 3538952 | tf_op jit(solution)/shard_map/ppermute | solution.py:22
  136.8 17.6 %collective-permute-start.13 = (bf16[384,768]{1,0:T(8,128)(2,1)S(1)}, bf16[384,768]{1,0:T(8,128)(2,1)S(1)}, u32[]{:S(2)}, u32[]{:S(2)}) collective-permute-start(bf16[384,768]{1,0:T(8,128)(2,1)S(1)} %bitcast.104), channel_id=1, source_target_pairs={{0,64},{64,0},{1,65},{65,1},{2,66},{66,2},{3,67},{67,3},{4,68},{68... | collective-permute-start | bytes 1769480 | tf_op jit(solution)/shard_map/ppermute | solution.py:22
  156.4 16.4 %collective-permute-start.14 = (bf16[768,768]{1,0:T(8,128)(2,1)}, bf16[768,768]{1,0:T(8,128)(2,1)}, u32[]{:S(2)}, u32[]{:S(2)}) collective-permute-start(bf16[768,768]{1,0:T(8,128)(2,1)} %pad_maximum_fusion.3), channel_id=1, source_target_pairs={{0,1},{1,0},{2,3},{3,2},{4,5},{5,4},{6,7},{7,6},{8,9},{9,8},{10,11... | collective-permute-start | bytes 3538952 | tf_op jit(solution)/shard_map/ppermute | solution.py:22
  163.2 21.6 %collective-permute-start.5 = (bf16[192,1024]{1,0:T(8,128)(2,1)S(1)}, bf16[192,1024]{1,0:T(8,128)(2,1)S(1)}, u32[]{:S(2)}, u32[]{:S(2)}) collective-permute-start(bf16[192,1024]{1,0:T(8,128)(2,1)S(1)} %get-tuple-element.11), channel_id=1, source_target_pairs={{0,2},{2,0},{4,6},{6,4},{1,3},{3,1},{5,7},{7,5},{8,10},{10,8},{12,... | collective-permute-start | bytes 1179656 | tf_op jit(solution)/shard_map/ppermute | solution.py:146
  166.2 29.7 %collective-permute-start.6 = (bf16[192,1024]{1,0:T(8,128)(2,1)S(1)}, bf16[192,1024]{1,0:T(8,128)(2,1)S(1)}, u32[]{:S(2)}, u32[]{:S(2)}) collective-permute-start(bf16[192,1024]{1,0:T(8,128)(2,1)S(1)} %get-tuple-element.13), channel_id=1, source_target_pairs={{0,4},{2,6},{4,0},{6,2},{1,5},{3,7},{5,1},{7,3},{8,12},{10,14},{12... | collective-permute-start | bytes 1179656 | tf_op jit(solution)/shard_map/ppermute | solution.py:146
  169.6 53.1 %collective-permute-start.7 = (bf16[192,1024]{1,0:T(8,128)(2,1)S(1)}, bf16[192,1024]{1,0:T(8,128)(2,1)S(1)}, u32[]{:S(2)}, u32[]{:S(2)}) collective-permute-start(bf16[192,1024]{1,0:T(8,128)(2,1)S(1)} %get-tuple-element.12), channel_id=1, source_target_pairs={{0,6},{2,4},{4,2},{6,0},{1,7},{3,5},{5,3},{7,1},{8,14},{10,12},{12... | collective-permute-start | bytes 1179656 | tf_op jit(solution)/shard_map/ppermute | solution.py:146
  177.5 51.9 %collective-permute-start.15 = (bf16[192,1024]{1,0:T(8,128)(2,1)S(1)}, bf16[192,1024]{1,0:T(8,128)(2,1)S(1)}, u32[]{:S(2)}, u32[]{:S(2)}) collective-permute-start(bf16[192,1024]{1,0:T(8,128)(2,1)S(1)} %get-tuple-element.14), channel_id=1, source_target_pairs={{0,2},{2,0},{4,6},{6,4},{1,3},{3,1},{5,7},{7,5},{8,10},{10,8},{12,... | collective-permute-start | bytes 1179656 | tf_op jit(solution)/shard_map/ppermute | solution.py:146
  181.4 50.9 %collective-permute-start.16 = (bf16[192,1024]{1,0:T(8,128)(2,1)S(1)}, bf16[192,1024]{1,0:T(8,128)(2,1)S(1)}, u32[]{:S(2)}, u32[]{:S(2)}) collective-permute-start(bf16[192,1024]{1,0:T(8,128)(2,1)S(1)} %get-tuple-element.16), channel_id=1, source_target_pairs={{0,4},{2,6},{4,0},{6,2},{1,5},{3,7},{5,1},{7,3},{8,12},{10,14},{12... | collective-permute-start | bytes 1179656 | tf_op jit(solution)/shard_map/ppermute | solution.py:146
  184.8 63.2 %collective-permute-start.17 = (bf16[192,1024]{1,0:T(8,128)(2,1)S(1)}, bf16[192,1024]{1,0:T(8,128)(2,1)S(1)}, u32[]{:S(2)}, u32[]{:S(2)}) collective-permute-start(bf16[192,1024]{1,0:T(8,128)(2,1)S(1)} %get-tuple-element.15), channel_id=1, source_target_pairs={{0,6},{2,4},{4,2},{6,0},{1,7},{3,5},{5,3},{7,1},{8,14},{10,12},{12... | collective-permute-start | bytes 1179656 | tf_op jit(solution)/shard_map/ppermute | solution.py:146
  223.1 27.3 %collective-permute-start.8 = (bf16[192,512]{1,0:T(8,128)(2,1)S(1)}, bf16[192,512]{1,0:T(8,128)(2,1)S(1)}, u32[]{:S(2)}, u32[]{:S(2)}) collective-permute-start(bf16[192,512]{1,0:T(8,128)(2,1)S(1)} %get-tuple-element.6), channel_id=1, source_target_pairs={{0,2},{2,0},{4,6},{6,4},{1,3},{3,1},{5,7},{7,5},{8,10},{10,8},{12,... | collective-permute-start | bytes 589832 | tf_op jit(solution)/shard_map/ppermute | solution.py:152
  225.1 25.7 %collective-permute-start.9 = (bf16[192,512]{1,0:T(8,128)(2,1)S(1)}, bf16[192,512]{1,0:T(8,128)(2,1)S(1)}, u32[]{:S(2)}, u32[]{:S(2)}) collective-permute-start(bf16[192,512]{1,0:T(8,128)(2,1)S(1)} %get-tuple-element.6), channel_id=1, source_target_pairs={{0,4},{2,6},{4,0},{6,2},{1,5},{3,7},{5,1},{7,3},{8,12},{10,14},{12... | collective-permute-start | bytes 589832 | tf_op jit(solution)/shard_map/ppermute | solution.py:152
  229.5 26.2 %collective-permute-start.10 = (bf16[192,512]{1,0:T(8,128)(2,1)S(1)}, bf16[192,512]{1,0:T(8,128)(2,1)S(1)}, u32[]{:S(2)}, u32[]{:S(2)}) collective-permute-start(bf16[192,512]{1,0:T(8,128)(2,1)S(1)} %get-tuple-element.6), channel_id=1, source_target_pairs={{0,6},{2,4},{4,2},{6,0},{1,7},{3,5},{5,3},{7,1},{8,14},{10,12},{12... | collective-permute-start | bytes 589832 | tf_op jit(solution)/shard_map/ppermute | solution.py:152
  248.5 14.4 %collective-permute-start.18 = (bf16[192,512]{1,0:T(8,128)(2,1)S(1)}, bf16[192,512]{1,0:T(8,128)(2,1)S(1)}, u32[]{:S(2)}, u32[]{:S(2)}) collective-permute-start(bf16[192,512]{1,0:T(8,128)(2,1)S(1)} %get-tuple-element.8), channel_id=1, source_target_pairs={{0,2},{2,0},{4,6},{6,4},{1,3},{3,1},{5,7},{7,5},{8,10},{10,8},{12,... | collective-permute-start | bytes 589832 | tf_op jit(solution)/shard_map/ppermute | solution.py:152
  255.7 25.3 %collective-permute-start.11 = (bf16[768,512]{1,0:T(8,128)(2,1)S(1)}, bf16[768,512]{1,0:T(8,128)(2,1)S(1)}, u32[]{:S(2)}, u32[]{:S(2)}) collective-permute-start(bf16[768,512]{1,0:T(8,128)(2,1)S(1)} %bitcast.102), channel_id=1, source_target_pairs={{0,1},{1,0},{2,3},{3,2},{4,5},{5,4},{6,7},{7,6},{8,9},{9,8},{10,11... | collective-permute-start | bytes 2359304 | tf_op jit(solution)/shard_map/ppermute | solution.py:22
  257.7 15.6 %collective-permute-start.19 = (bf16[192,512]{1,0:T(8,128)(2,1)S(1)}, bf16[192,512]{1,0:T(8,128)(2,1)S(1)}, u32[]{:S(2)}, u32[]{:S(2)}) collective-permute-start(bf16[192,512]{1,0:T(8,128)(2,1)S(1)} %get-tuple-element.8), channel_id=1, source_target_pairs={{0,4},{2,6},{4,0},{6,2},{1,5},{3,7},{5,1},{7,3},{8,12},{10,14},{12... | collective-permute-start | bytes 589832 | tf_op jit(solution)/shard_map/ppermute | solution.py:152
  259.6 19.5 %collective-permute-start.20 = (bf16[192,512]{1,0:T(8,128)(2,1)S(1)}, bf16[192,512]{1,0:T(8,128)(2,1)S(1)}, u32[]{:S(2)}, u32[]{:S(2)}) collective-permute-start(bf16[192,512]{1,0:T(8,128)(2,1)S(1)} %get-tuple-element.8), channel_id=1, source_target_pairs={{0,6},{2,4},{4,2},{6,0},{1,7},{3,5},{5,3},{7,1},{8,14},{10,12},{12... | collective-permute-start | bytes 589832 | tf_op jit(solution)/shard_map/ppermute | solution.py:152
  279.1 5.8 %collective-permute-start.21 = (bf16[768,512]{1,0:T(8,128)(2,1)S(1)}, bf16[768,512]{1,0:T(8,128)(2,1)S(1)}, u32[]{:S(2)}, u32[]{:S(2)}) collective-permute-start(bf16[768,512]{1,0:T(8,128)(2,1)S(1)} %bitcast.100), channel_id=1, source_target_pairs={{0,1},{1,0},{2,3},{3,2},{4,5},{5,4},{6,7},{7,6},{8,9},{9,8},{10,11... | collective-permute-start | bytes 2359304 | tf_op jit(solution)/shard_map/ppermute | solution.py:22
  282.7 17.6 %collective-permute-start.12 = (bf16[384,768]{1,0:T(8,128)(2,1)S(1)}, bf16[384,768]{1,0:T(8,128)(2,1)S(1)}, u32[]{:S(2)}, u32[]{:S(2)}) collective-permute-start(bf16[384,768]{1,0:T(8,128)(2,1)S(1)} %slice.157), channel_id=1, source_target_pairs={{0,64},{64,0},{1,65},{65,1},{2,66},{66,2},{3,67},{67,3},{4,68},{68... | collective-permute-start | bytes 1769480 | tf_op jit(solution)/shard_map/ppermute | solution.py:22
  301.3 26.9 %all-to-all-start.3 = ((bf16[8,48,768]{2,1,0:T(8,128)(2,1)}), bf16[8,48,768]{2,1,0:T(8,128)(2,1)S(1)}, u32[]{:S(2)}, u32[]{:S(2)}) async-start(bf16[8,48,768]{2,1,0:T(8,128)(2,1)} %bitcast.24), calls=%async_computation.3 | async-start | bytes 1179648 | tf_op jit(solution)/shard_map/all_to_all | solution.py:161
  310.7 56.4 %copy-start.10 = (f32[64]{0:T(128)S(1)}, f32[64]{0:T(128)}, u32[]{:S(2)}) copy-start(f32[64]{0:T(128)} %param.16) | copy-start | bytes 772
  310.7 16.6 %collective-permute-start.22 = (bf16[384,768]{1,0:T(8,128)(2,1)S(1)}, bf16[384,768]{1,0:T(8,128)(2,1)S(1)}, u32[]{:S(2)}, u32[]{:S(2)}) collective-permute-start(bf16[384,768]{1,0:T(8,128)(2,1)S(1)} %slice.156), channel_id=1, source_target_pairs={{0,64},{64,0},{1,65},{65,1},{2,66},{66,2},{3,67},{67,3},{4,68},{68... | collective-permute-start | bytes 1769480 | tf_op jit(solution)/shard_map/ppermute | solution.py:22
  328.2 24.2 %all-to-all-start.5 = ((bf16[8,48,768]{2,1,0:T(8,128)(2,1)}), bf16[8,48,768]{2,1,0:T(8,128)(2,1)S(1)}, u32[]{:S(2)}, u32[]{:S(2)}) async-start(bf16[8,48,768]{2,1,0:T(8,128)(2,1)} %bitcast.36), calls=%async_computation.5 | async-start | bytes 1179648 | tf_op jit(solution)/shard_map/all_to_all | solution.py:161
  (7 other events, 41.2 us)
where the time goes:
time: 369 us; the launch traced here: 368 us
  waiting for transfers between devices  187 us (51%)
  starting transfers between devices  97 us (26%)
  blocking collectives  44.6 us (12%)
  matrix products  19.7 us (5%)
  other arithmetic  10.2 us (3%)
  local copies, waits for them, and re-layouts  8.49 us (2%)
    ppermute x6, waiting for transfers between devices, body(): full = full + lax.ppermute(piece(i), 'yl', Y_XOR[i]).astype(F32)  51 us
    ppermute x9, waiting for transfers between devices, swap(): return lax.ppermute(x, axis, SWAP)  49.9 us
    ppermute x6, waiting for transfers between devices, body(): lax.ppermute(hidden, 'yl', Y_XOR[i])  21.5 us
    all_to_all x1, blocking collectives, body(): lax.all_to_all(packed, ('yh', 'xh'), split_axis=0, concat_axis=0, tiled=T...  20.1 us
    ppermute x6, starting transfers between devices, body(): full = full + lax.ppermute(piece(i), 'yl', Y_XOR[i]).astype(F32)  19.3 us
    ppermute x9, starting transfers between devices, swap(): return lax.ppermute(x, axis, SWAP)  18.1 us
    all_to_all x2, waiting for transfers between devices, body(): lax.all_to_all(jnp.broadcast_to(part[None], (nz, block, feat)), 'z', spli...  17.9 us
    all_to_all x2, waiting for transfers between devices, body(): lax.all_to_all(summed.reshape(nz, block, feat), 'z', split_axis=0, concat...  17.2 us
  transfers between devices with their start and end apart: 28, of which 16 were waited for; matrix products, arithmetic and copies ran while one was open for 7% of the time, Pallas kernels for 0%

commit v1 on v0

--- a/solution.py
+++ b/solution.py
@@ -99,7 +99,7 @@
     w_out_other = halves(w_down, 1 - core)
     attn = attend(queries, keys, values)
     mixed = residual.astype(F32) + attn.astype(F32)
-    total_squares = lax.psum(jnp.sum(mixed * mixed, axis=1), EXP)
+    total_squares = lax.psum(lax.psum(jnp.sum(mixed * mixed, axis=1), "c"), "yl")
     normed = (mixed * lax.rsqrt(total_squares / D + 1e-05)[:, None] * norm_gain[None, :]).astype(
         BF16
     )

time: 369 us -> 364 us (0.986)
  waiting for transfers between devices: 187 us -> 181 us
    ppermute x9, waiting for transfers between devices: 49.9 us -> 46.2 us  [swap(): return lax.ppermute(x, axis, SWAP)]
    psum x1 -> x2, blocking collectives: 10 us -> 10.9 us  [the longest x1 8.46 us: body(): lax.psum(lax.psum(jnp.sum(mixed * mixed, axis=1), 'c'), 'yl')]
  transfers between devices with their start and end apart: 28 -> 28, of which waited for: 16 -> 15; matrix products, arithmetic and copies ran while one was open for 7% -> 7% of each run, Pallas kernels for 0% -> 0%
where the time goes in v1:
time: 364 us; the launch traced here: 363 us
  waiting for transfers between devices  181 us (50%)
  starting transfers between devices  97.7 us (27%)
  blocking collectives  44.5 us (12%)
  matrix products  19.7 us (5%)
  other arithmetic  10.2 us (3%)
  local copies, waits for them, and re-layouts  8.61 us (2%)
    ppermute x6, waiting for transfers between devices, body(): full = full + lax.ppermute(piece(i), 'yl', Y_XOR[i]).astype(F32)  51 us
    ppermute x9, waiting for transfers between devices, swap(): return lax.ppermute(x, axis, SWAP)  46.2 us
    ppermute x6, waiting for transfers between devices, body(): lax.ppermute(hidden, 'yl', Y_XOR[i])  21.5 us
    ppermute x9, starting transfers between devices, swap(): return lax.ppermute(x, axis, SWAP)  19.6 us
    all_to_all x1, blocking collectives, body(): lax.all_to_all(packed, ('yh', 'xh'), split_axis=0, concat_axis=0, tiled=T...  19.2 us
    ppermute x6, starting transfers between devices, body(): full = full + lax.ppermute(piece(i), 'yl', Y_XOR[i]).astype(F32)  19.2 us
    all_to_all x2, waiting for transfers between devices, body(): lax.all_to_all(summed.reshape(nz, block, feat), 'z', split_axis=0, concat...  17.2 us
    all_to_all x1, waiting for transfers between devices, attend(): lax.all_to_all(jnp.broadcast_to(kv[None], (members,) + kv.shape), HALF, s...  15.9 us
  transfers between devices with their start and end apart: 28, of which 15 were waited for; matrix products, arithmetic and copies ran while one was open for 7% of the time, Pallas kernels for 0%

profile of v1, /device:TPU:8, one launch (start us, length us, event | category | flops | bytes accessed | tf_op | source)
XLA Modules:
  0.0 362.9 jit_solution(7593553249262115242)
XLA Ops:
  2.0 13.2 %all-to-all-start = ((bf16[32,64,256]{2,1,0:T(8,128)(2,1)}), bf16[32,64,256]{2,1,0:T(8,128)(2,1)S(1)}, u32[]{:S(2)}, u32[]{:S(2)}) async-start(bf16[32,64,256]{2,1,0:T(8,128)(2,1)} %broadcast_in_dim.68), calls=%async_computation | async-start | bytes 2097152 | tf_op jit(solution)/shard_map/all_to_all | solution.py:40
  17.1 10.6 %collective-permute-done = bf16[64,768]{1,0:T(8,128)(2,1)S(1)} collective-permute-done((bf16[64,768]{1,0:T(8,128)(2,1)S(1)}, bf16[64,768]{1,0:T(8,128)(2,1)S(1)}, u32[]{:S(2)}, u32[]{:S(2)}) %collective-permute-start) | collective-permute-done | bytes 98336 | tf_op jit(solution)/shard_map/ppermute | solution.py:37
  27.9 15.9 %all-to-all-done = bf16[32,64,256]{2,1,0:T(8,128)(2,1)S(1)} async-done(((bf16[32,64,256]{2,1,0:T(8,128)(2,1)}), bf16[32,64,256]{2,1,0:T(8,128)(2,1)S(1)}, u32[]{:S(2)}, u32[]{:S(2)}) %all-to-all-start) | async-done | bytes 1048608 | tf_op jit(solution)/shard_map/all_to_all | solution.py:40
  49.5 6.8 %collective-permute-start.1 = (bf16[64,896]{1,0:T(8,128)(2,1)S(1)}, bf16[64,896]{1,0:T(8,128)(2,1)S(1)}, u32[]{:S(2)}, u32[]{:S(2)}) collective-permute-start(bf16[64,896]{1,0:T(8,128)(2,1)S(1)} %fusion.34), channel_id=1, source_target_pairs={{0,256},{1,257},{2,258},{3,259},{4,260},{5,261},{6,262},{7,263},{8... | collective-permute-start | bytes 344072 | tf_op jit(solution)/shard_map/ppermute | solution.py:75
  56.6 3.2 collective-permute-done.1
  62.7 8.5 %psum.15 = f32[64]{0:T(128)S(1)} all-reduce(f32[64]{0:T(128)S(1)} %psum.14), channel_id=1, replica_groups=mesh['yh'=2,'xh'=2,'xl'=2,'z'=8,'yl'=4,'c'=2] {'yl'}, use_global_device_ids=true, to_apply=%region_6.7 | all-reduce | flops 64 | bytes 512 | tf_op jit(solution)/shard_map/psum | solution.py:102
  71.4 19.2 %all_to_all.35 = bf16[4,24,768]{2,1,0:T(8,128)(2,1)S(1)} all-to-all(bf16[4,24,768]{2,1,0:T(8,128)(2,1)S(1)} %convolution_convert_fusion), channel_id=1, replica_groups=mesh['yh'=2,'xh'=2,'xl'=2,'z'=8,'yl'=4,'c'=2] {'yh','xh'}, dimensions={0} | all-to-all | bytes 294912 | tf_op jit(solution)/shard_map/all_to_all | solution.py:116
  91.6 4.9 %all-to-all-start.2 = ((bf16[8,48,768]{2,1,0:T(8,128)(2,1)}), bf16[8,48,768]{2,1,0:T(8,128)(2,1)S(1)}, u32[]{:S(2)}, u32[]{:S(2)}) async-start(bf16[8,48,768]{2,1,0:T(8,128)(2,1)} %broadcast_in_dim.73), calls=%async_computation.2 | async-start | bytes 1179648 | tf_op jit(solution)/shard_map/all_to_all | solution.py:124
  96.6 15.8 %all-to-all-done.2 = bf16[8,48,768]{2,1,0:T(8,128)(2,1)S(1)} async-done(((bf16[8,48,768]{2,1,0:T(8,128)(2,1)}), bf16[8,48,768]{2,1,0:T(8,128)(2,1)S(1)}, u32[]{:S(2)}, u32[]{:S(2)}) %all-to-all-start.2) | async-done | bytes 589856 | tf_op jit(solution)/shard_map/all_to_all | solution.py:124
  113.2 3.5 all-to-all-start.4
  125.5 4.2 %collective-permute-done.2 = bf16[384,768]{1,0:T(8,128)(2,1)S(1)} collective-permute-done((bf16[384,768]{1,0:T(8,128)(2,1)S(1)}, bf16[384,768]{1,0:T(8,128)(2,1)S(1)}, u32[]{:S(2)}, u32[]{:S(2)}) %collective-permute-start.2) | collective-permute-done | bytes 589856 | tf_op jit(solution)/shard_map/ppermute | solution.py:22
  135.3 15.1 %collective-permute-done.13 = bf16[384,768]{1,0:T(8,128)(2,1)S(1)} collective-permute-done((bf16[384,768]{1,0:T(8,128)(2,1)S(1)}, bf16[384,768]{1,0:T(8,128)(2,1)S(1)}, u32[]{:S(2)}, u32[]{:S(2)}) %collective-permute-start.13) | collective-permute-done | bytes 589856 | tf_op jit(solution)/shard_map/ppermute | solution.py:22
  154.4 3.3 fusion.67
  159.2 3.5 collective-permute-start.5
  164.7 4.1 %collective-permute-start.7 = (bf16[192,1024]{1,0:T(8,128)(2,1)S(1)}, bf16[192,1024]{1,0:T(8,128)(2,1)S(1)}, u32[]{:S(2)}, u32[]{:S(2)}) collective-permute-start(bf16[192,1024]{1,0:T(8,128)(2,1)S(1)} %get-tuple-element.12), channel_id=1, source_target_pairs={{0,6},{2,4},{4,2},{6,0},{1,7},{3,5},{5,3},{7,1},{8,14},{10,12},{12... | collective-permute-start | bytes 1179656 | tf_op jit(solution)/shard_map/ppermute | solution.py:146
  168.8 3.2 fusion.68
  173.5 4.4 %collective-permute-start.15 = (bf16[192,1024]{1,0:T(8,128)(2,1)S(1)}, bf16[192,1024]{1,0:T(8,128)(2,1)S(1)}, u32[]{:S(2)}, u32[]{:S(2)}) collective-permute-start(bf16[192,1024]{1,0:T(8,128)(2,1)S(1)} %get-tuple-element.14), channel_id=1, source_target_pairs={{0,2},{2,0},{4,6},{6,4},{1,3},{3,1},{5,7},{7,5},{8,10},{10,8},{12,... | collective-permute-start | bytes 1179656 | tf_op jit(solution)/shard_map/ppermute | solution.py:146
  179.9 3.4 collective-permute-start.17
  183.2 7.8 %collective-permute-done.6 = bf16[192,1024]{1,0:T(8,128)(2,1)S(1)} collective-permute-done((bf16[192,1024]{1,0:T(8,128)(2,1)S(1)}, bf16[192,1024]{1,0:T(8,128)(2,1)S(1)}, u32[]{:S(2)}, u32[]{:S(2)}) %collective-permute-start.6) | collective-permute-done | bytes 393248 | tf_op jit(solution)/shard_map/ppermute | solution.py:146
  191.0 27.6 %collective-permute-done.7 = bf16[192,1024]{1,0:T(8,128)(2,1)S(1)} collective-permute-done((bf16[192,1024]{1,0:T(8,128)(2,1)S(1)}, bf16[192,1024]{1,0:T(8,128)(2,1)S(1)}, u32[]{:S(2)}, u32[]{:S(2)}) %collective-permute-start.7) | collective-permute-done | bytes 393248 | tf_op jit(solution)/shard_map/ppermute | solution.py:146
  221.0 3.5 collective-permute-start.9
  224.5 3.8 %collective-permute-start.10 = (bf16[192,512]{1,0:T(8,128)(2,1)S(1)}, bf16[192,512]{1,0:T(8,128)(2,1)S(1)}, u32[]{:S(2)}, u32[]{:S(2)}) collective-permute-start(bf16[192,512]{1,0:T(8,128)(2,1)S(1)} %get-tuple-element.6), channel_id=1, source_target_pairs={{0,6},{2,4},{4,2},{6,0},{1,7},{3,5},{5,3},{7,1},{8,14},{10,12},{12... | collective-permute-start | bytes 589832 | tf_op jit(solution)/shard_map/ppermute | solution.py:152
  228.4 15.6 %collective-permute-done.17 = bf16[192,1024]{1,0:T(8,128)(2,1)S(1)} collective-permute-done((bf16[192,1024]{1,0:T(8,128)(2,1)S(1)}, bf16[192,1024]{1,0:T(8,128)(2,1)S(1)}, u32[]{:S(2)}, u32[]{:S(2)}) %collective-permute-start.17) | collective-permute-done | bytes 393248 | tf_op jit(solution)/shard_map/ppermute | solution.py:146
  246.4 5.3 %collective-permute-done.10 = bf16[192,512]{1,0:T(8,128)(2,1)S(1)} collective-permute-done((bf16[192,512]{1,0:T(8,128)(2,1)S(1)}, bf16[192,512]{1,0:T(8,128)(2,1)S(1)}, u32[]{:S(2)}, u32[]{:S(2)}) %collective-permute-start.10) | collective-permute-done | bytes 196640 | tf_op jit(solution)/shard_map/ppermute | solution.py:152
  258.0 11.3 %collective-permute-done.19 = bf16[192,512]{1,0:T(8,128)(2,1)S(1)} collective-permute-done((bf16[192,512]{1,0:T(8,128)(2,1)S(1)}, bf16[192,512]{1,0:T(8,128)(2,1)S(1)}, u32[]{:S(2)}, u32[]{:S(2)}) %collective-permute-start.19) | collective-permute-done | bytes 196640 | tf_op jit(solution)/shard_map/ppermute | solution.py:152
  269.3 4.9 %collective-permute-done.20 = bf16[192,512]{1,0:T(8,128)(2,1)S(1)} collective-permute-done((bf16[192,512]{1,0:T(8,128)(2,1)S(1)}, bf16[192,512]{1,0:T(8,128)(2,1)S(1)}, u32[]{:S(2)}, u32[]{:S(2)}) %collective-permute-start.20) | collective-permute-done | bytes 196640 | tf_op jit(solution)/shard_map/ppermute | solution.py:152
  282.5 12.9 %collective-permute-done.12 = bf16[384,768]{1,0:T(8,128)(2,1)S(1)} collective-permute-done((bf16[384,768]{1,0:T(8,128)(2,1)S(1)}, bf16[384,768]{1,0:T(8,128)(2,1)S(1)}, u32[]{:S(2)}, u32[]{:S(2)}) %collective-permute-start.12) | collective-permute-done | bytes 589856 | tf_op jit(solution)/shard_map/ppermute | solution.py:22
  296.4 6.8 %all-to-all-start.3 = ((bf16[8,48,768]{2,1,0:T(8,128)(2,1)}), bf16[8,48,768]{2,1,0:T(8,128)(2,1)S(1)}, u32[]{:S(2)}, u32[]{:S(2)}) async-start(bf16[8,48,768]{2,1,0:T(8,128)(2,1)} %bitcast.24), calls=%async_computation.3 | async-start | bytes 1179648 | tf_op jit(solution)/shard_map/all_to_all | solution.py:161
  308.3 14.0 %collective-permute-done.22 = bf16[384,768]{1,0:T(8,128)(2,1)S(1)} collective-permute-done((bf16[384,768]{1,0:T(8,128)(2,1)S(1)}, bf16[384,768]{1,0:T(8,128)(2,1)S(1)}, u32[]{:S(2)}, u32[]{:S(2)}) %collective-permute-start.22) | collective-permute-done | bytes 589856 | tf_op jit(solution)/shard_map/ppermute | solution.py:22
  323.3 6.9 %all-to-all-start.5 = ((bf16[8,48,768]{2,1,0:T(8,128)(2,1)}), bf16[8,48,768]{2,1,0:T(8,128)(2,1)S(1)}, u32[]{:S(2)}, u32[]{:S(2)}) async-start(bf16[8,48,768]{2,1,0:T(8,128)(2,1)} %bitcast.36), calls=%async_computation.5 | async-start | bytes 1179648 | tf_op jit(solution)/shard_map/all_to_all | solution.py:161
  330.4 17.2 %all-to-all-done.5 = bf16[8,48,768]{2,1,0:T(8,128)(2,1)S(1)} async-done(((bf16[8,48,768]{2,1,0:T(8,128)(2,1)}), bf16[8,48,768]{2,1,0:T(8,128)(2,1)S(1)}, u32[]{:S(2)}, u32[]{:S(2)}) %all-to-all-start.5) | async-done | bytes 589856 | tf_op jit(solution)/shard_map/all_to_all | solution.py:161
  347.7 14.3 %all_to_all.36 = bf16[4,24,768]{2,1,0:T(8,128)(2,1)S(1)} all-to-all(bf16[4,24,768]{2,1,0:T(8,128)(2,1)S(1)} %pad_maximum_fusion.6), channel_id=1, replica_groups=mesh['yh'=2,'xh'=2,'xl'=2,'z'=8,'yl'=4,'c'=2] {'yh','xh'}, dimensions={0} | all-to-all | bytes 294912 | tf_op jit(solution)/shard_map/all_to_all | solution.py:166
  (128 shorter events, 67.4 us)
Async XLA Ops:
  0.0 276.1 %copy-start = (bf16[1024,768]{1,0:T(8,128)(2,1)S(1)}, bf16[1024,768]{1,0:T(8,128)(2,1)}, u32[]{:S(2)}) copy-start(bf16[1024,768]{1,0:T(8,128)(2,1)} %param.19) | copy-start | bytes 4718596
  0.0 16.6 %copy-start.9 = (s32[64,1]{0,1:T(1,128)S(1)}, s32[64,1]{0,1:T(1,128)}, u32[]{:S(2)}) copy-start(s32[64,1]{0,1:T(1,128)} %param.15) | copy-start | bytes 772
  2.0 41.8 %all-to-all-start = ((bf16[32,64,256]{2,1,0:T(8,128)(2,1)}), bf16[32,64,256]{2,1,0:T(8,128)(2,1)S(1)}, u32[]{:S(2)}, u32[]{:S(2)}) async-start(bf16[32,64,256]{2,1,0:T(8,128)(2,1)} %broadcast_in_dim.68), calls=%async_computation | async-start | bytes 2097152 | tf_op jit(solution)/shard_map/all_to_all | solution.py:40
  15.2 12.5 %collective-permute-start = (bf16[64,768]{1,0:T(8,128)(2,1)S(1)}, bf16[64,768]{1,0:T(8,128)(2,1)S(1)}, u32[]{:S(2)}, u32[]{:S(2)}) collective-permute-start(bf16[64,768]{1,0:T(8,128)(2,1)S(1)} %copy-done.7), channel_id=1, source_target_pairs={{256,0},{257,1},{258,2},{259,3},{260,4},{261,5},{262,6},{263,7},{2... | collective-permute-start | bytes 294920 | tf_op jit(solution)/shard_map/ppermute | solution.py:37
  49.1 22.1 %copy-start.8 = (f32[768]{0:T(1024)S(1)}, f32[768]{0:T(1024)}, u32[]{:S(2)}) copy-start(f32[768]{0:T(1024)} %param.14) | copy-start | bytes 9220
  49.5 10.4 %collective-permute-start.1 = (bf16[64,896]{1,0:T(8,128)(2,1)S(1)}, bf16[64,896]{1,0:T(8,128)(2,1)S(1)}, u32[]{:S(2)}, u32[]{:S(2)}) collective-permute-start(bf16[64,896]{1,0:T(8,128)(2,1)S(1)} %fusion.34), channel_id=1, source_target_pairs={{0,256},{1,257},{2,258},{3,259},{4,260},{5,261},{6,262},{7,263},{8... | collective-permute-start | bytes 344072 | tf_op jit(solution)/shard_map/ppermute | solution.py:75
  91.6 20.7 %all-to-all-start.2 = ((bf16[8,48,768]{2,1,0:T(8,128)(2,1)}), bf16[8,48,768]{2,1,0:T(8,128)(2,1)S(1)}, u32[]{:S(2)}, u32[]{:S(2)}) async-start(bf16[8,48,768]{2,1,0:T(8,128)(2,1)} %broadcast_in_dim.73), calls=%async_computation.2 | async-start | bytes 1179648 | tf_op jit(solution)/shard_map/all_to_all | solution.py:124
  113.2 19.5 %all-to-all-start.4 = ((bf16[8,48,768]{2,1,0:T(8,128)(2,1)}), bf16[8,48,768]{2,1,0:T(8,128)(2,1)S(1)}, u32[]{:S(2)}, u32[]{:S(2)}) async-start(bf16[8,48,768]{2,1,0:T(8,128)(2,1)} %broadcast_in_dim.79), calls=%async_computation.4 | async-start | bytes 1179648 | tf_op jit(solution)/shard_map/all_to_all | solution.py:124
  116.8 12.8 %collective-permute-start.2 = (bf16[384,768]{1,0:T(8,128)(2,1)S(1)}, bf16[384,768]{1,0:T(8,128)(2,1)S(1)}, u32[]{:S(2)}, u32[]{:S(2)}) collective-permute-start(bf16[384,768]{1,0:T(8,128)(2,1)S(1)} %bitcast.107), channel_id=1, source_target_pairs={{0,64},{64,0},{1,65},{65,1},{2,66},{66,2},{3,67},{67,3},{4,68},{68... | collective-permute-start | bytes 1769480 | tf_op jit(solution)/shard_map/ppermute | solution.py:22
  123.6 30.8 %collective-permute-start.4 = (bf16[1024,768]{1,0:T(8,128)(2,1)}, bf16[1024,768]{1,0:T(8,128)(2,1)}, u32[]{:S(2)}, u32[]{:S(2)}) collective-permute-start(bf16[1024,768]{1,0:T(8,128)(2,1)} %pad_maximum_fusion.1), channel_id=1, source_target_pairs={{0,1},{1,0},{2,3},{3,2},{4,5},{5,4},{6,7},{7,6},{8,9},{9,8},{10,11... | collective-permute-start | bytes 4718600 | tf_op jit(solution)/shard_map/ppermute | solution.py:22
  130.9 23.5 %collective-permute-start.3 = (bf16[768,768]{1,0:T(8,128)(2,1)}, bf16[768,768]{1,0:T(8,128)(2,1)}, u32[]{:S(2)}, u32[]{:S(2)}) collective-permute-start(bf16[768,768]{1,0:T(8,128)(2,1)} %pad_maximum_fusion.2), channel_id=1, source_target_pairs={{0,1},{1,0},{2,3},{3,2},{4,5},{5,4},{6,7},{7,6},{8,9},{9,8},{10,11... | collective-permute-start | bytes 3538952 | tf_op jit(solution)/shard_map/ppermute | solution.py:22
  132.8 17.6 %collective-permute-start.13 = (bf16[384,768]{1,0:T(8,128)(2,1)S(1)}, bf16[384,768]{1,0:T(8,128)(2,1)S(1)}, u32[]{:S(2)}, u32[]{:S(2)}) collective-permute-start(bf16[384,768]{1,0:T(8,128)(2,1)S(1)} %bitcast.104), channel_id=1, source_target_pairs={{0,64},{64,0},{1,65},{65,1},{2,66},{66,2},{3,67},{67,3},{4,68},{68... | collective-permute-start | bytes 1769480 | tf_op jit(solution)/shard_map/ppermute | solution.py:22
  152.4 16.4 %collective-permute-start.14 = (bf16[768,768]{1,0:T(8,128)(2,1)}, bf16[768,768]{1,0:T(8,128)(2,1)}, u32[]{:S(2)}, u32[]{:S(2)}) collective-permute-start(bf16[768,768]{1,0:T(8,128)(2,1)} %pad_maximum_fusion.3), channel_id=1, source_target_pairs={{0,1},{1,0},{2,3},{3,2},{4,5},{5,4},{6,7},{7,6},{8,9},{9,8},{10,11... | collective-permute-start | bytes 3538952 | tf_op jit(solution)/shard_map/ppermute | solution.py:22
  159.2 20.6 %collective-permute-start.5 = (bf16[192,1024]{1,0:T(8,128)(2,1)S(1)}, bf16[192,1024]{1,0:T(8,128)(2,1)S(1)}, u32[]{:S(2)}, u32[]{:S(2)}) collective-permute-start(bf16[192,1024]{1,0:T(8,128)(2,1)S(1)} %get-tuple-element.11), channel_id=1, source_target_pairs={{0,2},{2,0},{4,6},{6,4},{1,3},{3,1},{5,7},{7,5},{8,10},{10,8},{12,... | collective-permute-start | bytes 1179656 | tf_op jit(solution)/shard_map/ppermute | solution.py:146
  162.7 28.3 %collective-permute-start.6 = (bf16[192,1024]{1,0:T(8,128)(2,1)S(1)}, bf16[192,1024]{1,0:T(8,128)(2,1)S(1)}, u32[]{:S(2)}, u32[]{:S(2)}) collective-permute-start(bf16[192,1024]{1,0:T(8,128)(2,1)S(1)} %get-tuple-element.13), channel_id=1, source_target_pairs={{0,4},{2,6},{4,0},{6,2},{1,5},{3,7},{5,1},{7,3},{8,12},{10,14},{12... | collective-permute-start | bytes 1179656 | tf_op jit(solution)/shard_map/ppermute | solution.py:146
  164.7 54.0 %collective-permute-start.7 = (bf16[192,1024]{1,0:T(8,128)(2,1)S(1)}, bf16[192,1024]{1,0:T(8,128)(2,1)S(1)}, u32[]{:S(2)}, u32[]{:S(2)}) collective-permute-start(bf16[192,1024]{1,0:T(8,128)(2,1)S(1)} %get-tuple-element.12), channel_id=1, source_target_pairs={{0,6},{2,4},{4,2},{6,0},{1,7},{3,5},{5,3},{7,1},{8,14},{10,12},{12... | collective-permute-start | bytes 1179656 | tf_op jit(solution)/shard_map/ppermute | solution.py:146
  173.5 51.0 %collective-permute-start.15 = (bf16[192,1024]{1,0:T(8,128)(2,1)S(1)}, bf16[192,1024]{1,0:T(8,128)(2,1)S(1)}, u32[]{:S(2)}, u32[]{:S(2)}) collective-permute-start(bf16[192,1024]{1,0:T(8,128)(2,1)S(1)} %get-tuple-element.14), channel_id=1, source_target_pairs={{0,2},{2,0},{4,6},{6,4},{1,3},{3,1},{5,7},{7,5},{8,10},{10,8},{12,... | collective-permute-start | bytes 1179656 | tf_op jit(solution)/shard_map/ppermute | solution.py:146
  177.9 50.4 %collective-permute-start.16 = (bf16[192,1024]{1,0:T(8,128)(2,1)S(1)}, bf16[192,1024]{1,0:T(8,128)(2,1)S(1)}, u32[]{:S(2)}, u32[]{:S(2)}) collective-permute-start(bf16[192,1024]{1,0:T(8,128)(2,1)S(1)} %get-tuple-element.16), channel_id=1, source_target_pairs={{0,4},{2,6},{4,0},{6,2},{1,5},{3,7},{5,1},{7,3},{8,12},{10,14},{12... | collective-permute-start | bytes 1179656 | tf_op jit(solution)/shard_map/ppermute | solution.py:146
  179.9 64.1 %collective-permute-start.17 = (bf16[192,1024]{1,0:T(8,128)(2,1)S(1)}, bf16[192,1024]{1,0:T(8,128)(2,1)S(1)}, u32[]{:S(2)}, u32[]{:S(2)}) collective-permute-start(bf16[192,1024]{1,0:T(8,128)(2,1)S(1)} %get-tuple-element.15), channel_id=1, source_target_pairs={{0,6},{2,4},{4,2},{6,0},{1,7},{3,5},{5,3},{7,1},{8,14},{10,12},{12... | collective-permute-start | bytes 1179656 | tf_op jit(solution)/shard_map/ppermute | solution.py:146
  219.1 27.3 %collective-permute-start.8 = (bf16[192,512]{1,0:T(8,128)(2,1)S(1)}, bf16[192,512]{1,0:T(8,128)(2,1)S(1)}, u32[]{:S(2)}, u32[]{:S(2)}) collective-permute-start(bf16[192,512]{1,0:T(8,128)(2,1)S(1)} %get-tuple-element.6), channel_id=1, source_target_pairs={{0,2},{2,0},{4,6},{6,4},{1,3},{3,1},{5,7},{7,5},{8,10},{10,8},{12,... | collective-permute-start | bytes 589832 | tf_op jit(solution)/shard_map/ppermute | solution.py:152
  221.0 25.4 %collective-permute-start.9 = (bf16[192,512]{1,0:T(8,128)(2,1)S(1)}, bf16[192,512]{1,0:T(8,128)(2,1)S(1)}, u32[]{:S(2)}, u32[]{:S(2)}) collective-permute-start(bf16[192,512]{1,0:T(8,128)(2,1)S(1)} %get-tuple-element.6), channel_id=1, source_target_pairs={{0,4},{2,6},{4,0},{6,2},{1,5},{3,7},{5,1},{7,3},{8,12},{10,14},{12... | collective-permute-start | bytes 589832 | tf_op jit(solution)/shard_map/ppermute | solution.py:152
  224.5 27.2 %collective-permute-start.10 = (bf16[192,512]{1,0:T(8,128)(2,1)S(1)}, bf16[192,512]{1,0:T(8,128)(2,1)S(1)}, u32[]{:S(2)}, u32[]{:S(2)}) collective-permute-start(bf16[192,512]{1,0:T(8,128)(2,1)S(1)} %get-tuple-element.6), channel_id=1, source_target_pairs={{0,6},{2,4},{4,2},{6,0},{1,7},{3,5},{5,3},{7,1},{8,14},{10,12},{12... | collective-permute-start | bytes 589832 | tf_op jit(solution)/shard_map/ppermute | solution.py:152
  244.4 13.5 %collective-permute-start.18 = (bf16[192,512]{1,0:T(8,128)(2,1)S(1)}, bf16[192,512]{1,0:T(8,128)(2,1)S(1)}, u32[]{:S(2)}, u32[]{:S(2)}) collective-permute-start(bf16[192,512]{1,0:T(8,128)(2,1)S(1)} %get-tuple-element.8), channel_id=1, source_target_pairs={{0,2},{2,0},{4,6},{6,4},{1,3},{3,1},{5,7},{7,5},{8,10},{10,8},{12,... | collective-permute-start | bytes 589832 | tf_op jit(solution)/shard_map/ppermute | solution.py:152
  251.7 24.4 %collective-permute-start.11 = (bf16[768,512]{1,0:T(8,128)(2,1)S(1)}, bf16[768,512]{1,0:T(8,128)(2,1)S(1)}, u32[]{:S(2)}, u32[]{:S(2)}) collective-permute-start(bf16[768,512]{1,0:T(8,128)(2,1)S(1)} %bitcast.102), channel_id=1, source_target_pairs={{0,1},{1,0},{2,3},{3,2},{4,5},{5,4},{6,7},{7,6},{8,9},{9,8},{10,11... | collective-permute-start | bytes 2359304 | tf_op jit(solution)/shard_map/ppermute | solution.py:22
  253.6 15.6 %collective-permute-start.19 = (bf16[192,512]{1,0:T(8,128)(2,1)S(1)}, bf16[192,512]{1,0:T(8,128)(2,1)S(1)}, u32[]{:S(2)}, u32[]{:S(2)}) collective-permute-start(bf16[192,512]{1,0:T(8,128)(2,1)S(1)} %get-tuple-element.8), channel_id=1, source_target_pairs={{0,4},{2,6},{4,0},{6,2},{1,5},{3,7},{5,1},{7,3},{8,12},{10,14},{12... | collective-permute-start | bytes 589832 | tf_op jit(solution)/shard_map/ppermute | solution.py:152
  255.6 18.6 %collective-permute-start.20 = (bf16[192,512]{1,0:T(8,128)(2,1)S(1)}, bf16[192,512]{1,0:T(8,128)(2,1)S(1)}, u32[]{:S(2)}, u32[]{:S(2)}) collective-permute-start(bf16[192,512]{1,0:T(8,128)(2,1)S(1)} %get-tuple-element.8), channel_id=1, source_target_pairs={{0,6},{2,4},{4,2},{6,0},{1,7},{3,5},{5,3},{7,1},{8,14},{10,12},{12... | collective-permute-start | bytes 589832 | tf_op jit(solution)/shard_map/ppermute | solution.py:152
  274.2 6.1 %collective-permute-start.21 = (bf16[768,512]{1,0:T(8,128)(2,1)S(1)}, bf16[768,512]{1,0:T(8,128)(2,1)S(1)}, u32[]{:S(2)}, u32[]{:S(2)}) collective-permute-start(bf16[768,512]{1,0:T(8,128)(2,1)S(1)} %bitcast.100), channel_id=1, source_target_pairs={{0,1},{1,0},{2,3},{3,2},{4,5},{5,4},{6,7},{7,6},{8,9},{9,8},{10,11... | collective-permute-start | bytes 2359304 | tf_op jit(solution)/shard_map/ppermute | solution.py:22
  277.8 17.6 %collective-permute-start.12 = (bf16[384,768]{1,0:T(8,128)(2,1)S(1)}, bf16[384,768]{1,0:T(8,128)(2,1)S(1)}, u32[]{:S(2)}, u32[]{:S(2)}) collective-permute-start(bf16[384,768]{1,0:T(8,128)(2,1)S(1)} %slice.157), channel_id=1, source_target_pairs={{0,64},{64,0},{1,65},{65,1},{2,66},{66,2},{3,67},{67,3},{4,68},{68... | collective-permute-start | bytes 1769480 | tf_op jit(solution)/shard_map/ppermute | solution.py:22
  296.4 26.9 %all-to-all-start.3 = ((bf16[8,48,768]{2,1,0:T(8,128)(2,1)}), bf16[8,48,768]{2,1,0:T(8,128)(2,1)S(1)}, u32[]{:S(2)}, u32[]{:S(2)}) async-start(bf16[8,48,768]{2,1,0:T(8,128)(2,1)} %bitcast.24), calls=%async_computation.3 | async-start | bytes 1179648 | tf_op jit(solution)/shard_map/all_to_all | solution.py:161
  305.7 56.3 %copy-start.10 = (f32[64]{0:T(128)S(1)}, f32[64]{0:T(128)}, u32[]{:S(2)}) copy-start(f32[64]{0:T(128)} %param.16) | copy-start | bytes 772
  305.7 16.6 %collective-permute-start.22 = (bf16[384,768]{1,0:T(8,128)(2,1)S(1)}, bf16[384,768]{1,0:T(8,128)(2,1)S(1)}, u32[]{:S(2)}, u32[]{:S(2)}) collective-permute-start(bf16[384,768]{1,0:T(8,128)(2,1)S(1)} %slice.156), channel_id=1, source_target_pairs={{0,64},{64,0},{1,65},{65,1},{2,66},{66,2},{3,67},{67,3},{4,68},{68... | collective-permute-start | bytes 1769480 | tf_op jit(solution)/shard_map/ppermute | solution.py:22
  323.3 24.2 %all-to-all-start.5 = ((bf16[8,48,768]{2,1,0:T(8,128)(2,1)}), bf16[8,48,768]{2,1,0:T(8,128)(2,1)S(1)}, u32[]{:S(2)}, u32[]{:S(2)}) async-start(bf16[8,48,768]{2,1,0:T(8,128)(2,1)} %bitcast.36), calls=%async_computation.5 | async-start | bytes 1179648 | tf_op jit(solution)/shard_map/all_to_all | solution.py:161
  (7 other events, 42.2 us)
